TPU v7x, 32 devices: a whole 2x2x4 slice. The times are simulated.
32 devices in a mesh: dp: 16 (over z, x, core), band: 2 (over y).
Axes of the slice: x: 2, y: 2, z: 4, core: 2. Of those that a mesh axis runs over, the one named last changes fastest.
Arguments:
- block_input: bfloat16 [16, 5, 32, 16, 1024], P('dp', None, 'band'), may hold values from -6 to 6
- modulation: float32 [16, 6, 1024], P('dp'), may hold values from -2 to 2
- band_live: int32 [16, 2], P('dp'), may hold values 0 or 1
- w_query: bfloat16 [1024, 1024], replicated, may hold values from -0.25 to 0.25
- w_key: bfloat16 [1024, 1024], replicated, may hold values from -0.25 to 0.25
- w_value: bfloat16 [1024, 1024], replicated, may hold values from -0.1875 to 0.1875
- w_out: bfloat16 [1024, 1024], replicated, may hold values from -0.5 to 0.5
- w_up: bfloat16 [1024, 4096], replicated, may hold values from -0.1875 to 0.1875
- w_down: bfloat16 [4096, 1024], replicated, may hold values from -0.09375 to 0.09375
- cotangent: bfloat16 [16, 5, 32, 16, 1024], P('dp', None, 'band'), may hold values from -6 to 6
Outputs:
- block_output: bfloat16 [16, 5, 32, 16, 1024], P('dp', None, 'band')
- grad_input: bfloat16 [16, 5, 32, 16, 1024], P('dp', None, 'band')
- grad_modulation: float32 [16, 6, 1024], P('dp')
- grad_w_query: float32 [1048576], P('dp')
- grad_w_key: float32 [1048576], P('dp')
- grad_w_value: float32 [1048576], P('dp')
- grad_w_out: float32 [1048576], P('dp')
- grad_w_up: float32 [4194304], P('dp')
- grad_w_down: float32 [4194304], P('dp')
Inputs may be any that keep to these rules, and one draw needn't show every extreme that they name: band_live[c, b] is 1 where band b of clip c holds latent rows and 0 where that band slot is empty; an empty band's tokens pass the block unchanged.
All inputs are finite; a program needn't handle non-finite values.
Results may differ from a plain program's by a relative error of at most 0.015.
The roundings to bfloat16 on the way count: a program that leaves them out, or rounds other values in their place, can miss the bound.
Values may be sent and summed in bfloat16 or wider, within the bound.
A program may use at most 384 MiB of HBM per device.

v0:
```python
import functools

import jax
import jax.numpy as jnp
from jax import lax
from jax.experimental import pallas as pl
from jax.experimental.pallas import tpu as pltpu
from jax.sharding import PartitionSpec as P

HEADS = 16
HEAD_DIM = 64
EPS = 1e-06
MASKED = -1e30
LOG2E = 1.4426950408889634
F32 = jnp.float32
BF16 = jnp.bfloat16
ANY = pl.BlockSpec(memory_space=pl.ANY)
VMEM_LIMIT = 60 * 1024 * 1024

MID_SPOTS = ((1, 0), (2, 0), (1, 1), (2, 1))


def group_spot(band, s):
    lone = 3 * band
    paired = 3 - 3 * band
    if s < 2:
        return lone, s
    if s < 6:
        return MID_SPOTS[s - 2]
    return paired, s - 6


def params(limit=VMEM_LIMIT, **kw):
    return pltpu.CompilerParams(vmem_limit_bytes=limit, **kw)


def dot(a, b, ca=1, cb=0):
    return lax.dot_general(a, b, (((ca,), (cb,)), ((), ())), preferred_element_type=F32)


def whole(shape):
    return pl.BlockSpec(shape, lambda *_: (0,) * len(shape), pipeline_mode=pl.Buffered(1))


def norm_stats(v):
    c = v - jnp.mean(v, axis=-1, keepdims=True)
    r = lax.rsqrt(jnp.mean(c * c, axis=-1, keepdims=True) + EPS)
    return c * r, r


def spot_copy(hbm, vmem, band, s, sem, out=False):
    g, j = group_spot(band, s)
    there = hbm.at[0, :, pl.ds(g * 4, 4), pl.ds(j * 8, 8), :]
    if out:
        slot = s % vmem.shape[0]
        return pltpu.make_async_copy(vmem.at[slot], there, sem.at[slot])
    return pltpu.make_async_copy(there, vmem.at[s], sem.at[s])


def pre_kernel(n_group, from_spots, x_hbm, mod_ref, *refs):
    n_mat = (len(refs) - 5) // 2 if from_spots else (len(refs) - 3) // 2
    w_refs = refs[:n_mat]
    outs = refs[n_mat:]
    if from_spots:
        xw_ref, normed_ref = outs[:2]
        o_refs = outs[2 : 2 + n_mat]
    else:
        o_refs = outs[:n_mat]
    stage, sem, nsc = outs[-3:] if not from_spots else outs[-3:]
    rows = nsc.shape[0] // n_group

    @pl.when(pl.program_id(0) == 0)
    def _():
        band = lax.axis_index("band")
        if from_spots:
            copies = [spot_copy(x_hbm, stage, band, s, sem) for s in range(n_group)]
        else:
            copies = [
                pltpu.make_async_copy(x_hbm.at[:, :, pl.ds(8 * s, 8), :], stage.at[s], sem.at[s])
                for s in range(n_group)
            ]
        for c in copies:
            c.start()
        for s in range(n_group):
            copies[s].wait()
            x = stage[s].astype(F32).reshape(rows, stage.shape[-1])
            n, _ = norm_stats(x)
            part = pl.ds(s * rows, rows)
            nsc[part, :] = (n * (1.0 + mod_ref[1:2, :]) + mod_ref[0:1, :]).astype(BF16)
            if from_spots:
                xw_ref[part, :] = x.astype(BF16)
        if from_spots:
            normed_ref[...] = jnp.transpose(nsc[...])

    for w_ref, o_ref in zip(w_refs, o_refs):
        o_ref[...] = dot(nsc[...], w_ref[...]).astype(BF16)


def pre(x, mod, weights, n_group, from_spots):
    d = x.shape[-1]
    frames = x.shape[1] if from_spots else x.shape[0]
    rows = frames * 32
    t = n_group * rows
    tile = 256
    o_tile = pl.BlockSpec((t, tile), lambda n: (0, n))
    full = pl.BlockSpec((t, d), lambda n: (0, 0))
    act = jax.ShapeDtypeStruct((t, d), BF16)
    k = len(weights)
    head = [act, jax.ShapeDtypeStruct((d, t), BF16)] if from_spots else []
    return pl.pallas_call(
        functools.partial(pre_kernel, n_group, from_spots),
        grid=(d // tile,),
        in_specs=[ANY, whole((6, d))] + [pl.BlockSpec((d, tile), lambda n: (0, n))] * k,
        out_specs=[full, whole((d, t))][: len(head)] + [o_tile] * k,
        out_shape=head + [act] * k,
        scratch_shapes=[
            pltpu.VMEM((n_group, frames, 4, 8, d), BF16),
            pltpu.SemaphoreType.DMA((n_group,)),
            pltpu.VMEM((t, d), BF16),
        ],
        compiler_params=params(),
        name="pre" if from_spots else "pre_halo",
        cost_estimate=pl.CostEstimate(
            flops=2 * t * d * d * k, bytes_accessed=2 * (k * d * d + (k + 3) * t * d), transcendentals=0
        ),
    )(x, mod, *weights)


LANES = 512


class Reduce:
    def __init__(self, dp, total_rows, orders, tiles_only):
        self.bits = list(range(dp.bit_length() - 2, 0, -1))
        self.nz = len(self.bits)
        self.stages = self.nz + 1
        self.depth = self.stages + 4
        self.r = total_rows // dp
        self.orders = orders
        self.tiles_only = tiles_only
        self.dp = dp

    def scratch(self):
        r, nz, k = self.r, self.nz, self.stages
        out = [] if self.tiles_only else [pltpu.VMEM((1 << nz, r, LANES), BF16)]
        out += [pltpu.VMEM((2, 1 << nz, r, LANES), BF16)]
        for _ in range(2):
            for i in range(k):
                block = (2,) * (k - 1 - i) + (r, 128)
                out += [pltpu.VMEM(block, BF16), pltpu.VMEM(block, BF16), pltpu.VMEM((2,) + block, BF16)]
        out += [pltpu.VMEM((2, r, 128), BF16), pltpu.VMEM((2, 2, r, 128), BF16), pltpu.VMEM((r, LANES), F32)]
        out += [pltpu.SemaphoreType.DMA((2 * k + 4,)), pltpu.SemaphoreType.DMA((2 * k + 2, 2))]
        return out

    def bind(self, refs, jobs, tiles):
        refs = list(refs)
        cube = (2,) * self.nz
        self.own = tiles.at[0, :, 0] if self.tiles_only else refs.pop(0)
        self.got_core = refs.pop(0)
        self.got_cube = self.got_core.reshape((2,) + cube + (self.r, LANES))
        if self.tiles_only:
            self.tile_cube = tiles.reshape((2,) + cube + (2, self.r, LANES))
        else:
            self.own_cube = self.own.reshape(cube + (self.r, LANES))
        self.send, self.keep, self.got = {}, {}, {}
        for p in range(2):
            for i in range(self.stages):
                self.send[p, i], self.keep[p, i], self.got[p, i] = refs.pop(0), refs.pop(0), refs.pop(0)
        self.fin, self.got_fin, self.ostage, self.ssem, self.rsem = refs
        self.jobs = jobs
        self.starts = [job[0] for job in jobs]
        self.me, self.band = lax.axis_index("dp"), lax.axis_index("band")

    def place(self, axis):
        return self.band if axis == 0 else lax.rem(self.me // (1 << axis), 2)

    def partner(self, axis):
        if axis == 0:
            return (self.me, 1 - self.band)
        bit = 1 if axis == -1 else 1 << axis
        here = lax.rem(self.me // bit, 2)
        return (self.me + bit - 2 * bit * here, self.band)

    def barrier(self):
        sem = pltpu.get_barrier_semaphore()
        everyone = [-1, 0] + self.bits
        for axis in everyone:
            pl.semaphore_signal(sem, inc=1, device_id=self.partner(axis), device_id_type=pl.DeviceIdType.MESH)
        pl.semaphore_wait(sem, len(everyone))

    def remote(self, src, dst, s, slot, axis):
        return pltpu.make_async_remote_copy(
            src_ref=src,
            dst_ref=dst,
            send_sem=self.ssem.at[s],
            recv_sem=self.rsem.at[s, slot],
            device_id=self.partner(axis),
            device_id_type=pl.DeviceIdType.MESH,
        )

    def core_copy(self, slot, src):
        return self.remote(src, self.got_core.at[slot], 2 * self.stages, slot, -1)

    def part_copy(self, p, i, slot):
        return self.remote(self.send[p, i], self.got[p, i].at[slot], 2 * i + p, slot, self.orders[p][i])

    def fin_copy(self, slot):
        return self.remote(self.fin, self.got_fin.at[slot], 2 * self.stages + 1, slot, 0)

    def pick(self, axes, axis, at):
        return tuple(at if a == axis else slice(None) for a in axes)

    def split_core(self, j, p):
        slot = lax.rem(j, 2)
        first = self.orders[p][0]
        mine = self.place(first)
        for dst, at in ((self.send[p, 0], 1 - mine), (self.keep[p, 0], mine)):
            if first == 0:
                lanes = pl.ds(pl.multiple_of((2 * p + at) * 128, 128), 128)
                idx = (slice(None),) * (self.nz + 1) + (lanes,)
                dst[...] = self.mine(slot, idx) + self.got_cube[(slot,) + idx]
            else:
                for b in range(2):
                    lanes = slice((2 * p + b) * 128, (2 * p + b + 1) * 128)
                    idx = self.pick(self.bits, first, at) + (slice(None), lanes)
                    dst[(slice(None),) * (self.nz - 1) + (b,)] = self.mine(slot, idx) + self.got_cube[(slot,) + idx]

    def split(self, j, p, i):
        slot = lax.rem(j, 2)
        axes = [a for a in self.bits + [0] if a not in self.orders[p][:i]]
        axis = self.orders[p][i]
        mine = self.place(axis)
        for dst, at in ((self.send[p, i], 1 - mine), (self.keep[p, i], mine)):
            idx = self.pick(axes, axis, at)
            dst[...] = self.keep[p, i - 1][idx] + self.got[p, i - 1][(slot,) + idx]

    def stage(self, s, j):
        k = self.stages
        slot = lax.rem(j, 2)
        if s == 0:
            self.each(j, 1)
        elif s == 1:
            self.core_copy(slot, self.own).wait()
            if not self.tiles_only:
                self.own_copy(self.own).wait()
            for p in range(2):
                self.split_core(j, p)
                self.part_copy(p, 0, slot).start()
        elif s <= k:
            for p in range(2):
                self.part_copy(p, s - 2, slot).wait()
                self.split(j, p, s - 1)
                self.part_copy(p, s - 1, slot).start()
        elif s == k + 1:
            for p in range(2):
                self.part_copy(p, k - 1, slot).wait()
                self.fin[p] = self.keep[p, k - 1][...] + self.got[p, k - 1][slot]
            self.fin_copy(slot).start()
        elif s == k + 2:
            self.fin_copy(slot).wait()
            for p in range(2):
                mine = pl.ds(pl.multiple_of((2 * p + self.band) * 128, 128), 128)
                other = pl.ds(pl.multiple_of((2 * p + 1 - self.band) * 128, 128), 128)
                self.ostage[:, mine] = self.fin[p].astype(F32)
                self.ostage[:, other] = self.got_fin[slot, p].astype(F32)
            self.each(j, 2)
        else:
            self.out_copy(self.ostage).wait()

    def each(self, j, part):
        for i, job in enumerate(self.jobs):
            pl.when(j == i)(functools.partial(job[part], self, i % 2))

    def own_copy(self, src):
        return pltpu.make_async_copy(src, self.own, self.ssem.at[2 * self.stages + 2])

    def out_copy(self, dst, src=None):
        return pltpu.make_async_copy(self.ostage if src is None else src, dst, self.ssem.at[2 * self.stages + 3])

    def mine(self, slot, idx):
        if self.tiles_only:
            return self.tile_cube[(slot,) + idx[: self.nz] + (lax.rem(self.me, 2),) + idx[self.nz :]]
        return self.own_cube[idx]

    def start_pair(self, slot, ref, at):
        core = lax.rem(self.me, 2)
        if not self.tiles_only:
            self.own_copy(ref.at[(slice(None), core) + at]).start()
        self.core_copy(slot, ref.at[(slice(None), 1 - core) + at]).start()

    def tick(self, t):
        for s in reversed(range(self.depth)):
            u = t - s
            before = sum(jnp.where(u > at, 1, 0) for at in self.starts)
            upto = sum(jnp.where(u >= at, 1, 0) for at in self.starts)

            @pl.when(upto > before)
            def _():
                self.stage(s, before)

    def plain(self, src, dst, send_sem, recv_sem, axis):
        return pltpu.make_async_remote_copy(
            src_ref=src,
            dst_ref=dst,
            send_sem=send_sem,
            recv_sem=recv_sem,
            device_id=self.partner(axis),
            device_id_type=pl.DeviceIdType.MESH,
        )


def cube_shape(red, rows, cols):
    return (red.dp // 2, 2, rows // (red.r * red.dp), red.r, cols)


def lanes_at(i, width=LANES):
    return slice(i * width, (i + 1) * width)


def array_job(start, src, dst, q, i, q_out=None):
    def begin(red, slot):
        red.start_pair(slot, src, (q, slice(None), lanes_at(i)))

    def end(red, slot):
        red.out_copy(dst.at[q if q_out is None else q_out, :, lanes_at(i)]).start()

    return start, begin, end


def tile_job(start, tiles, at, parts):
    width = LANES // len(parts)

    def begin(red, slot):
        red.start_pair(slot, tiles.at[at], ())

    def end(red, slot):
        for n, dst in enumerate(parts):
            red.out_copy(dst, red.ostage.at[:, lanes_at(n, width)]).start()

    return start, begin, end


def tile_scratch(red):
    return pltpu.VMEM((2, red.dp // 2, 2, red.r, LANES), BF16)


def put_tile(red, tiles, slot, v):
    tiles[slot] = v.reshape(tiles.shape[1:]).astype(BF16)


SCALE = HEAD_DIM**-0.5
SCALE2 = SCALE * LOG2E


def head_masks(rows):
    left = lax.broadcasted_iota(jnp.int32, (rows, 128), 1) < 64
    return left, jnp.logical_not(left)


def only(mask, v):
    return jnp.where(mask, v, jnp.zeros_like(v))


def each_window(r, body):
    for first, rows, at, shared in ((4, r, 6 * r, True), (0, r, 0, False), (2, 2 * r, 2 * r, False)):
        yield functools.partial(window_pair, r, first, rows, at, shared, body)


def window_pair(r, first, rows, at, shared, body):
    def one(i, _):
        q0 = pl.multiple_of(at + i * rows, 32)
        k0 = pl.multiple_of(2 * r * i, 32) if shared else q0
        body(first + i, i, pl.ds(q0, rows), pl.ds(k0, 2 * r if shared else rows), shared)
        return 0

    lax.fori_loop(0, 2, one, 0)


def fill_shared(scratch, own_ref, halo_ref, r):
    for w in range(2):
        scratch[2 * r * w : 2 * r * w + r, :] = own_ref[(6 + w) * r : (7 + w) * r, :]
        scratch[2 * r * w + r : 2 * r * (w + 1), :] = halo_ref[r * w : r * (w + 1), :]


def attn_fwd_kernel(ok_ref, q_ref, k_ref, v_ref, kh_ref, vh_ref, o_ref, lse_ref, kc, vc):
    r = q_ref.shape[0] // 8
    fill_shared(kc, k_ref, kh_ref, r)
    fill_shared(vc, v_ref, vh_ref, r)
    col = lax.broadcasted_iota(jnp.int32, (1, 2 * r), 1)
    bias = jnp.where((col >= r) & (ok_ref[0] != 1), MASKED, 0.0)
    for w, (q0, qn) in enumerate(((0, r), (r, r), (2 * r, 2 * r), (4 * r, 2 * r), (6 * r, r), (7 * r, r))):
        rows = slice(q0, q0 + qn)
        q = q_ref[rows, :]
        if w < 4:
            k, v = k_ref[rows, :], v_ref[rows, :]
        else:
            keys = slice(2 * r * (w - 4), 2 * r * (w - 3))
            k, v = kc[keys, :], vc[keys, :]
        masks = head_masks(qn)
        o, lse = [], []
        for mask in masks:
            s = dot(only(mask, q), k, 1, 1) * SCALE2
            if w >= 4:
                s = s + bias
            top = jnp.max(s, axis=-1, keepdims=True)
            e = jnp.exp2(s - top)
            total = jnp.sum(e, axis=-1, keepdims=True)
            o.append(dot(e.astype(BF16), v) * (1.0 / total))
            lse.append(top + jnp.log2(total))
        o_ref[rows, :] = jnp.where(masks[0], o[0], o[1]).astype(BF16)
        turned = jnp.transpose(jnp.where(masks[0], lse[0], lse[1]))
        for h in range(2):
            lse_ref[w, h : h + 1, :qn] = turned[64 * h : 64 * h + 1, :]


def lse_lanes(t):
    return pl.cdiv(t // 4, 128) * 128


def attn_fwd(halo_ok, q, k, v, kh, vh):
    t, d = q.shape
    th = kh.shape[0]
    big = pl.BlockSpec((t, 128), lambda n: (0, n))
    small = pl.BlockSpec((th, 128), lambda n: (0, n))
    return pl.pallas_call(
        attn_fwd_kernel,
        grid=(d // 128,),
        in_specs=[pl.BlockSpec(memory_space=pltpu.SMEM), big, big, big, small, small],
        out_specs=[big, pl.BlockSpec((None, 6, 8, lse_lanes(t)), lambda n: (n, 0, 0, 0))],
        out_shape=[jax.ShapeDtypeStruct((t, d), BF16), jax.ShapeDtypeStruct((d // 128, 6, 8, lse_lanes(t)), F32)],
        scratch_shapes=[pltpu.VMEM((2 * th, 128), BF16)] * 2,
        compiler_params=params(),
        name="attn_fwd",
        cost_estimate=pl.CostEstimate(flops=t * t * d, bytes_accessed=12 * t * d, transcendentals=t * t * 3),
    )(halo_ok, q, k, v, kh, vh)


def mid_kernel(
    g_hbm, live_ref, att_ref, w_ref, x_ref, mod_ref, ao_ref, mid_ref, nm_ref, nmt_ref, attt_ref, gw_ref, gm_ref, stage, sem
):
    step = pl.program_id(0)
    band = lax.axis_index("band")
    live = live_ref[0].astype(F32)
    n_group = stage.shape[0]
    rows = gw_ref.shape[0] // n_group

    @pl.when(step == 0)
    def _():
        for s in range(n_group):
            spot_copy(g_hbm, stage, band, s, sem).start()

    attn_out = dot(att_ref[...], w_ref[...])
    middle = x_ref[...].astype(F32) + (live * mod_ref[2:3, :]) * attn_out
    ao_ref[...] = attn_out.astype(BF16)
    mid_ref[...] = middle
    n, _ = norm_stats(middle)
    nm = (n * (1.0 + mod_ref[4:5, :]) + mod_ref[3:4, :]).astype(BF16)
    nm_ref[...] = nm
    nmt_ref[...] = jnp.transpose(nm)
    attt_ref[...] = jnp.transpose(att_ref[...])
    for k in range(4):

        @pl.when(step == k + 1)
        def _():
            for s in range(2 * k, 2 * k + 2):
                spot_copy(g_hbm, stage, band, s, sem).wait()
                g = stage[s].astype(F32).reshape(rows, stage.shape[-1])
                part = slice(s * rows, (s + 1) * rows)
                gw_ref[part, :] = g.astype(BF16)
                gm_ref[part, :] = ((live * mod_ref[5:6, :]) * g).astype(BF16)


def mid(cot, live, attended, w_out, xw, mod):
    t, d = xw.shape
    frames = cot.shape[1]
    blk = pl.BlockSpec((t // 5, d), lambda m: (m, 0))
    blk_t = pl.BlockSpec((d, t // 5), lambda m: (0, m))
    full = pl.BlockSpec((t, d), lambda m: (0, 0))
    bf, f32 = jax.ShapeDtypeStruct((t, d), BF16), jax.ShapeDtypeStruct((t, d), F32)
    bf_t = jax.ShapeDtypeStruct((d, t), BF16)
    return pl.pallas_call(
        mid_kernel,
        grid=(5,),
        in_specs=[ANY, pl.BlockSpec(memory_space=pltpu.SMEM), blk, whole((d, d)), blk, whole((6, d))],
        out_specs=[blk, blk, blk, blk_t, blk_t, full, full],
        out_shape=[bf, f32, bf, bf_t, bf_t, bf, bf],
        scratch_shapes=[pltpu.VMEM((8, frames, 4, 8, d), BF16), pltpu.SemaphoreType.DMA((8,))],
        compiler_params=params(),
        name="mid",
        cost_estimate=pl.CostEstimate(flops=2 * t * d * d, bytes_accessed=22 * t * d, transcendentals=0),
    )(cot, live, attended, w_out, xw, mod)


GELU_C = 0.7978845608
GELU_A = 0.044715


def col_sum(v):
    return jnp.sum(v, axis=0, keepdims=True)


def norm_back(h, n, r, gain):
    e = h * (1.0 + gain)
    return r * (e - jnp.mean(e, axis=-1, keepdims=True) - n * jnp.mean(e * n, axis=-1, keepdims=True))


def add_sums(ref, first, rows):
    sums = jnp.concatenate(rows + [jnp.zeros((ref.shape[0] - len(rows), ref.shape[1]), F32)], axis=0)

    @pl.when(first)
    def _():
        ref[...] = sums

    @pl.when(jnp.logical_not(first))
    def _():
        ref[...] += sums


def put_groups(out, stage, out_hbm, sem, block, blocks):
    band = lax.axis_index("band")
    slots = stage.shape[0]
    n_group = 8
    per = n_group // blocks
    rows = out.shape[0] // per
    for k in range(blocks):

        @pl.when(block == k)
        def _():
            for i in range(per):
                s = k * per + i
                if s >= slots:
                    spot_copy(out_hbm, stage, band, s - slots, sem, out=True).wait()
                stage[s % slots] = out[i * rows : (i + 1) * rows, :].reshape(stage.shape[1:]).astype(BF16)
                spot_copy(out_hbm, stage, band, s, sem, out=True).start()

    @pl.when(block == blocks - 1)
    def _():
        for s in range(n_group - slots, n_group):
            spot_copy(out_hbm, stage, band, s, sem, out=True).wait()


PIECES = 4


class Tiling:
    def __init__(self, ff, dp):
        self.steps = ff // LANES
        self.width = LANES // PIECES
        self.early = ff // dp == 2 * self.width

    def piece(self, i, k):
        if not self.early:
            return PIECES * i + k
        half = self.steps // 2
        return (i % half * PIECES + k) * 2 + i // half


def window_back(w, rows, keys, bias, q_ref, k_ref, v_ref, do, lse_ref):
    q, k, v = q_ref[rows, :], k_ref[keys, :], v_ref[keys, :]
    kt = jnp.transpose(k)
    dq, dk, dv = [], [], []
    for h, mask in enumerate(head_masks(rows.size)):
        s = dot(k, only(mask, q), 1, 1) * SCALE2
        if bias is not None:
            s = s + bias
        p = jnp.exp2(s - lse_ref[w, h : h + 1, : rows.size])
        dp = dot(v, only(mask, do), 1, 1)
        total = jnp.sum(p * dp, axis=0, keepdims=True)
        ds = (p * (dp - total)).astype(BF16)
        dv.append(dot(p.astype(BF16), do))
        dk.append(dot(ds, q))
        dq.append(dot(kt[64 * h : 64 * h + 64, :], ds))
    left = head_masks(keys.size)[0]
    dq = jnp.transpose(jnp.concatenate(dq, axis=0)) * SCALE
    return dq, jnp.where(left, dk[0], dk[1]) * SCALE, jnp.where(left, dv[0], dv[1])


TILES = ((("q", 0), ("k", 0)), (("v", 0), ("v", 1)), (("q", 1), ("k", 1)), (("q", 2), ("k", 2)), (("v", 2), ("v", 3)), (("q", 3), ("k", 3)))
TILE_SLOTS = (0, 0, 1, 0, 1, 0)
MADE = {2: (0,), 4: (1, 2), 6: (3,), 8: (4, 5)}


class Plan:
    def __init__(self, n_ff, n_att, early):
        self.n_ff, self.n_att = n_ff, n_att
        self.post = n_ff
        self.out = n_ff + 4
        self.att = self.out + 1
        self.fin = self.att + n_att
        self.steps = self.fin + 4
        self.end = self.fin + 8
        a = self.att
        self.up = [(0, i + 1) for i in range(n_ff)]
        self.o_proj = [(0, a), (1, a)]
        self.tiles = [(1, a + 3), (1, a + 5), (0, a + 5), (1, a + 7), (1, self.fin + 1), (0, self.fin + 1)]
        late = [(1, n_ff + 1 + i) for i in range(4)]
        self.down = [(1, n_ff // 2 + 1 + i) for i in range(4)] + late if early else late + [(1, a + i) for i in (1, 2, 4, 6)]


def finish(reds, first):
    def body(u, _):
        for red in reds:
            red.tick(u)
        return 0

    lax.fori_loop(first, max(red.starts[-1] + red.depth for red in reds), body, 0)


def core_kernel(
    til, plan, reds, live_ref, ok_ref, nm_hbm, gm_hbm, nmt_hbm, attt_hbm, ndt_hbm, wu_hbm, wo_hbm, wq_hbm,
    wd_ref, mid_ref, g_ref, ao_ref, mod_ref, wk_ref, wv_ref, q_ref, k_ref, v_ref, lse_ref, kh_ref, vh_ref, x_ref,
    out_hbm, gin_hbm, sums_ref, sums_a_ref, dwd_hbm, gup_hbm, gdown_hbm, gout_hbm, gq_hbm, gk_hbm, gv_hbm,
    buf_a, buf_b, buf_c, buf_t, mo, h, do_s, w0, wu, dwd, tiles, kc, vc, own, hsend, hrecv,
    hsem, wsem, lsem, stage, sem, *scratch,
):
    step, steps = pl.program_id(0), pl.num_programs(0)
    n_ff, n_att, width = plan.n_ff, plan.n_att, til.width
    t, d = mo.shape
    chunk = t // 4
    r = t // 8
    red = reds[0]

    def up_at(i, k):
        return pl.ds(pl.multiple_of(til.piece(i, k) * width, width), width)

    def load_up(i, k):
        slot = lax.rem(i, 2)
        return pltpu.make_async_copy(wu_hbm.at[:, up_at(i, k)], wu.at[slot, :, lanes_at(k, width)], wsem.at[slot, k])

    def store_down(i, k):
        if til.early:
            d_at = til.piece(i, k) // 2
            dst = dwd_hbm.at[d_at // 2, lax.rem(d_at, 2), pl.ds(2 * lax.rem(til.piece(i, k), 2), 2)]
        else:
            dst = dwd_hbm.at[pl.ds(til.piece(i, k) * width, width), :]
        return pltpu.make_async_copy(dwd.at[k], dst, wsem.at[2, k])

    def load(n):
        pairs = ((nm_hbm, buf_b), (gm_hbm, buf_c), (nmt_hbm, buf_t), (wo_hbm, w0), (attt_hbm, buf_t), (ndt_hbm, buf_t), (wq_hbm, w0))
        return pltpu.make_async_copy(*pairs[n], lsem.at[n])

    grad_of = {"q": (buf_a, gq_hbm), "k": (buf_b, gk_hbm), "v": (buf_c, gv_hbm)}
    cube = dwd_hbm if til.early else dwd_hbm.reshape(cube_shape(red, dwd_hbm.shape[0], d))
    wide = d // LANES
    jobs = ([], [])
    for i, (at, start) in enumerate(plan.up):
        jobs[at].append(tile_job(start, tiles, i % 2, [gup_hbm.at[:, lanes_at(til.piece(i, k), width)] for k in range(PIECES)]))
    for n, (at, start) in enumerate(plan.down):
        jobs[at].append(array_job(start, cube, gdown_hbm, n // wide, n % wide))
    for n, (at, start) in enumerate(plan.o_proj):
        jobs[at].append(tile_job(start, tiles, n, [gout_hbm.at[:, lanes_at(n)]]))
    for m, (at, start) in enumerate(plan.tiles):
        jobs[at].append(tile_job(start, tiles, TILE_SLOTS[m], [grad_of[n][1].at[:, lanes_at(i, 256)] for n, i in TILES[m]]))
    size = len(scratch) // 2
    for i in range(2):
        reds[i].bind(scratch[i * size : (i + 1) * size + i], sorted(jobs[i], key=lambda job: job[0]), tiles)

    def swap(i):
        slot = lax.rem(i, 2)
        return red.plain(hsend, hrecv.at[slot], hsem.at[0], hsem.at[1 + slot], 0)

    @pl.when(step == 0)
    def _():
        for k in range(PIECES):
            load_up(0, k).start()
        for n in range(4):
            load(n).start()
        mo[...] = jnp.zeros_like(mo)
        h[...] = jnp.zeros_like(h)
        red.barrier()
        load(0).wait()
        load(1).wait()

    for one in reds:
        one.tick(step + jnp.maximum(step - plan.fin, 0))

    @pl.when(step < n_ff)
    def _():
        slot = lax.rem(step, 2)
        for k in range(PIECES):
            load_up(step, k).wait()

        @pl.when(step + 1 < n_ff)
        def _():
            for k in range(PIECES):
                load_up(step + 1, k).start()

        wd = wd_ref[...].reshape(LANES, d)
        up = wu.at[slot]

        def rows(i, _):
            part = pl.ds(pl.multiple_of(i * chunk, chunk), chunk)
            v = dot(buf_b[part, :], up[...])
            gh = dot(buf_c[part, :], wd, 1, 1)
            v2 = v * v
            th = jnp.tanh(v * (GELU_C + (GELU_C * GELU_A) * v2))
            half = 0.5 * th + 0.5
            hidden = (v * half).astype(BF16)
            slope = half + (0.5 * v) * (1.0 - th * th) * (GELU_C + (3.0 * GELU_C * GELU_A) * v2)
            gpre = (gh * slope).astype(BF16)
            buf_a[part, :LANES] = hidden
            buf_a[part, LANES : 2 * LANES] = gpre
            mo[part, :] += dot(hidden, wd)
            h[part, :] += dot(gpre, up[...], 1, 1)
            return 0

        lax.fori_loop(0, 4, rows, 0)

        @pl.when(step > 0)
        def _():
            for k in range(PIECES):
                store_down(step - 1, k).wait()

        pl.when(step == 0)(lambda: load(2).wait())
        put_tile(red, tiles, slot, dot(buf_t[...], buf_a[:, LANES : 2 * LANES]))
        dwd[...] = dot(buf_a[:, :LANES], buf_c[...], 0, 0).reshape(dwd.shape).astype(BF16)
        for k in range(PIECES):
            store_down(step, k).start()

    @pl.when((step >= plan.post) & (step < plan.out))
    def _():
        block = step - plan.post

        @pl.when(block == 0)
        def _():
            load(4).start()
            load(3).wait()
            for k in range(PIECES):
                store_down(step - 1, k).wait()

        part = pl.ds(pl.multiple_of(block * chunk, chunk), chunk)
        live = live_ref[0].astype(F32)
        middle, g = mid_ref[...], g_ref[...].astype(F32)
        mlp_out, hh = mo[part, :], h[part, :]
        n, rs = norm_stats(middle)
        gmid = g + norm_back(hh, n, rs, mod_ref[4:5, :])
        h[part, :] = gmid
        ga = ((live * mod_ref[2:3, :]) * gmid).astype(BF16)
        buf_b[part, :] = ga
        do_s[part, :] = dot(ga, w0[...], 1, 1).astype(BF16)
        sums = [col_sum(live * ao_ref[...].astype(F32) * gmid), col_sum(hh), col_sum(hh * n), col_sum(live * mlp_out * g)]
        add_sums(sums_ref, block == 0, sums)
        put_groups(middle + (live * mod_ref[5:6, :]) * mlp_out, stage, out_hbm, sem, block, 4)

    @pl.when(step == plan.out)
    def _():
        load(6).start()
        load(4).wait()
        for n in range(wide):
            put_tile(red, tiles, n, dot(buf_t[...], buf_b[:, lanes_at(n)]))
        load(5).start()

    now = step - plan.att

    @pl.when((now > 0) & (now <= n_att))
    def _():
        swap(now - 1).wait()
        slot = lax.rem(now - 1, 2)
        lanes = pl.ds(pl.multiple_of((now - 1) * 128, 128), 128)
        for i, ref in enumerate((buf_b, buf_c)):
            ref[6 * r :, lanes] = (own[i] + hrecv[slot, i].astype(F32)).astype(BF16)

    for at, made in MADE.items():

        @pl.when(now == at)
        def _():
            if at == min(MADE):
                load(5).wait()
            for m in made:
                cols = [grad_of[n][0][:, lanes_at(i, 256)] for n, i in TILES[m]]
                put_tile(red, tiles, TILE_SLOTS[m], dot(buf_t[...], jnp.concatenate(cols, axis=1)))

    @pl.when((now >= 0) & (now < n_att))
    def _():
        slot = lax.rem(now, 2)
        lanes = pl.ds(pl.multiple_of(now * 128, 128), 128)
        fill_shared(kc, k_ref, kh_ref, r)
        fill_shared(vc, v_ref, vh_ref, r)
        row = lax.broadcasted_iota(jnp.int32, (2 * r, 1), 0)
        bias = jnp.where((row >= r) & (ok_ref[0] != 1), MASKED, 0.0)

        def window(w, i, rows, keys, shared):
            data = (bias, q_ref, kc, vc) if shared else (None, q_ref, k_ref, v_ref)
            dq, dk, dv = window_back(w, rows, keys, *data, do_s[rows, lanes], lse_ref)
            buf_a[rows, lanes] = dq.astype(BF16)
            if shared:
                part = pl.ds(pl.multiple_of(i * r, 32), r)
                for n, v in enumerate((dk, dv)):
                    own[n, part, :] = v[:r, :]
                    hsend[n, part, :] = v[r:, :].astype(BF16)
            else:
                buf_b[rows, lanes] = dk.astype(BF16)
                buf_c[rows, lanes] = dv.astype(BF16)

        pairs = list(each_window(r, window))
        pairs[0]()
        swap(now).start()
        pairs[1]()
        pairs[2]()

    @pl.when(step >= plan.fin)
    def _():
        i = step - plan.fin
        pl.when(i == 0)(lambda: load(6).wait())
        part = pl.ds(pl.multiple_of(i * chunk, chunk), chunk)
        hh = dot(buf_a[part, :], w0[...], 1, 1) + dot(buf_b[part, :], wk_ref[...], 1, 1)
        for one in reds:
            one.tick(plan.fin + 2 * i + 1)
        hh = hh + dot(buf_c[part, :], wv_ref[...], 1, 1)
        n, rs = norm_stats(x_ref[...].astype(F32))
        add_sums(sums_a_ref, i == 0, [col_sum(hh), col_sum(hh * n)])
        put_groups(h[part, :] + norm_back(hh, n, rs, mod_ref[1:2, :]), stage, gin_hbm, sem, i, 4)

    @pl.when(step == steps - 1)
    def _():
        finish(reds, plan.end)


def core(live, halo_ok, nm, gm, nmt, attt, ndt, w_up, w_down, wo, wq, wk, wv, middle, gw, ao, mod, q, k, v, lse, kh, vh, xw, like):
    t, d = nm.shape
    ff = w_up.shape[1]
    th = kh.shape[0]
    frames = like.shape[1]
    dp = lax.axis_size("dp")
    til = Tiling(ff, dp)
    n_ff, n_att = til.steps, d // 128
    plan = Plan(n_ff, n_att, til.early)
    rest = tuple(range(3, dp.bit_length() - 1))
    reds = [Reduce(dp, d, ((0, 1, 2, *rest), (1, 2, 0, *rest)), i == 0) for i in range(2)]
    red = reds[0]

    def block_at(first, count):
        return lambda i: (jnp.clip(i - first, 0, count - 1), 0)

    def lane_at(i):
        return 0, jnp.clip(i - plan.att, 0, n_att - 1)

    post = pl.BlockSpec((t // 4, d), block_at(plan.post, 4))
    last = pl.BlockSpec((t // 4, d), block_at(plan.fin, 4), pipeline_mode=pl.Buffered(1))
    big, small = pl.BlockSpec((t, 128), lane_at), pl.BlockSpec((th, 128), lane_at)
    lse_spec = pl.BlockSpec((None, 6, 8, lse_lanes(t)), lambda i: (lane_at(i)[1], 0, 0, 0))
    if til.early:
        half = n_ff // 2
        w_down = w_down.reshape(half, PIECES, 2, til.width, d)

        def down_at(i):
            i = jnp.minimum(i, n_ff - 1)
            return lax.rem(i, half), 0, i // half, 0, 0

        down = pl.BlockSpec((None, PIECES, None, til.width, d), down_at)
        cube, down_tile = cube_shape(red, ff, d), (PIECES, 2, red.r, d)
    else:
        down = pl.BlockSpec((LANES, d), block_at(0, n_ff))
        cube, down_tile = (ff, d), (PIECES, til.width, d)
    smem = pl.BlockSpec(memory_space=pltpu.SMEM)
    full = pl.BlockSpec((8, d), lambda i: (0, 0))
    image, sums = jax.ShapeDtypeStruct(like.shape, BF16), jax.ShapeDtypeStruct((8, d), F32)
    share = jax.ShapeDtypeStruct((red.r, d), F32)
    act, act32 = pltpu.VMEM((t, d), BF16), pltpu.VMEM((t, d), F32)
    return pl.pallas_call(
        functools.partial(core_kernel, til, plan, reds),
        grid=(plan.steps,),
        in_specs=[smem, smem] + [ANY] * 8 + [down, post, post, post, whole((6, d)), whole((d, d)), whole((d, d))]
        + [big] * 3 + [lse_spec] + [small] * 2 + [last],
        out_specs=[ANY, ANY, full, full] + [ANY] * 7,
        out_shape=[image, image, sums, sums, jax.ShapeDtypeStruct(cube, BF16), jax.ShapeDtypeStruct((red.r, ff), F32)]
        + [jax.ShapeDtypeStruct((ff // d, red.r, d), F32), share, share, share, share],
        scratch_shapes=[
            act,
            act,
            act,
            pltpu.VMEM((d, t), BF16),
            act32,
            act32,
            act,
            pltpu.VMEM((d, d), BF16),
            pltpu.VMEM((2, d, LANES), BF16),
            pltpu.VMEM(down_tile, BF16),
            tile_scratch(red),
            pltpu.VMEM((2 * th, 128), BF16),
            pltpu.VMEM((2 * th, 128), BF16),
            pltpu.VMEM((2, th, 128), F32),
            pltpu.VMEM((2, th, 128), BF16),
            pltpu.VMEM((2, 2, th, 128), BF16),
            pltpu.SemaphoreType.DMA((3,)),
            pltpu.SemaphoreType.DMA((3, PIECES)),
            pltpu.SemaphoreType.DMA((7,)),
            pltpu.VMEM((4, frames, 4, 8, d), BF16),
            pltpu.SemaphoreType.DMA((4,)),
        ]
        + reds[0].scratch()
        + reds[1].scratch(),
        compiler_params=params(limit=63 * 1024 * 1024, collective_id=1, has_side_effects=True),
        name="core",
        cost_estimate=pl.CostEstimate(
            flops=12 * t * d * (ff + d) + 3 * t * t * d, bytes_accessed=8 * d * ff + 60 * t * d, transcendentals=t * (ff + 3 * t)
        ),
    )(live, halo_ok, nm, gm, nmt, attt, ndt, w_up, wo, wq, w_down, middle, gw, ao, mod, wk, wv, q, k, v, lse, kh, vh, xw)


def band_swap(v):
    return lax.ppermute(v, "band", [(0, 1), (1, 0)])


def on_device(
    block_input, modulation, band_live, w_query, w_key, w_value, w_out, w_up, w_down, cotangent
):
    assert lax.axis_size("band") == 2 and block_input.shape[2:4] == (16, 16)
    band = lax.axis_index("band")
    flags = band_live[0]
    live_own = lax.dynamic_index_in_dim(flags, band, keepdims=True)
    live_other = lax.dynamic_index_in_dim(flags, 1 - band, keepdims=True)
    live = (live_own == 1).astype(jnp.int32)
    halo_ok = ((live_other == 1) | (live_own != 1)).astype(jnp.int32)
    mod = modulation[0]

    edge = lax.dynamic_slice_in_dim(block_input[0], 12 - 12 * band, 4, axis=1)
    x_halo = band_swap(edge)
    xw, ndt, q, k, v = pre(block_input, mod, (w_query, w_key, w_value), 8, True)
    kh, vh = pre(x_halo, mod, (w_key, w_value), 2, False)
    attended, lse = attn_fwd(halo_ok, q, k, v, kh, vh)
    ao, middle, nm, nmt, attt, gw, gm = mid(cotangent, live, attended, w_out, xw, mod)
    block_output, grad_input, sums_m, sums_a, _, g_up, g_down, g_out, g_query, g_key, g_value = core(
        live, halo_ok, nm, gm, nmt, attt, ndt, w_up, w_down, w_out, w_query, w_key, w_value,
        middle, gw, ao, mod, q, k, v, lse, kh, vh, xw, block_input,
    )
    mod_part = jnp.concatenate([sums_a[0:2], sums_m[0:4]])
    mod_total = mod_part + band_swap(mod_part)
    grads = (g_query, g_key, g_value, g_out, g_up, g_down)
    return block_output, grad_input, mod_total[None], *(g.reshape(-1) for g in grads)


def solution(mesh):
    return jax.shard_map(
        on_device,
        mesh=mesh,
        in_specs=(
            P("dp", None, "band", None, None),
            P("dp", None, None),
            P("dp", None),
            P(),
            P(),
            P(),
            P(),
            P(),
            P(),
            P("dp", None, "band", None, None),
        ),
        out_specs=(
            P("dp", None, "band", None, None),
            P("dp", None, "band", None, None),
            P("dp", None, None),
            P("dp"),
            P("dp"),
            P("dp"),
            P("dp"),
            P("dp"),
            P("dp"),
        ),
        check_vma=False,
    )
```

profile of v0, /device:TPU:0, one launch (start us, length us, event | category | flops | bytes accessed | tf_op | source)
XLA Modules:
  0.0 321.8 jit_solution(4451148906944030326)
XLA Ops:
  0.6 1.1 dynamic-slice_bitcast_fusion
  1.8 3.0 collective-permute-start
  4.8 1.3 constant_dynamic-slice_fusion
  8.1 1.4 copy.28
  9.5 15.8 %pre.1 = (bf16[1280,1024]{1,0:T(8,128)(2,1)}, bf16[1024,1280]{1,0:T(8,128)(2,1)}, bf16[1280,1024]{1,0:T(8,128)(2,1)}, bf16[1280,1024]{1,0:T(8,128)(2,1)}, bf16[1280,1024]{1,0:T(8,128)(2,1)}) custom-call(bf16[1,5,16,16,1024]{4,3,2,1,0:T(8,128)(2,1)} %x_hbm.1, f32[6,1024]{1,0:T(8,128)} %bitcast.34, bf16[1024,1024]{1,0:T(8,128)(2,1)} %wq_hbm.1, ...), custom_call_target="tpu_custom_call" | custom-call | flops 8053063680 | bytes 22020096 | tf_op jit(solution)/shard_map/pre/pallas_call | solution.py:110
  25.2 0.0 collective-permute-done.x_hbm
  25.2 0.0 copy-start.4
  25.2 0.8 copy-done.4
  26.1 6.6 %pre_halo.1 = (bf16[320,1024]{1,0:T(8,128)(2,1)}, bf16[320,1024]{1,0:T(8,128)(2,1)}) custom-call(bf16[5,4,16,1024]{3,2,1,0:T(8,128)(2,1)} %copy-done.4, f32[6,1024]{1,0:T(8,128)} %bitcast.35, bf16[1024,1024]{1,0:T(8,128)(2,1)} %wk_ref.1, bf16[1024,1024]{1,0:T(8,128)(2,1)} %wv_ref.1), custom_call_target="tpu_custom_call" | custom-call | flops 1342177280 | bytes 7471104 | tf_op jit(solution)/shard_map/pre_halo/pallas_call | solution.py:110
  32.7 27.7 %attn_fwd.1 = (bf16[1280,1024]{1,0:T(8,128)(2,1)}, f32[8,6,8,384]{3,2,1,0:T(8,128)}) custom-call(s32[1]{0:T(128)} %bitcast.1.ok_ref, bf16[1280,1024]{1,0:T(8,128)(2,1)} %get-tuple-element.35.q_ref, bf16[1280,1024]{1,0:T(8,128)(2,1)} %get-tuple-element.36.k_ref, bf16[1280,1024]{1,0:T(8,128)(2,1)} %get-tuple-element.37.v_ref, ...), custom_call_target="tpu_custom_call" | custom-call | flops 1677721600 | bytes 15728640 | tf_op jit(solution)/shard_map/attn_fwd/pallas_call | solution.py:425
  60.5 13.3 %mid.1 = (bf16[1280,1024]{1,0:T(8,128)(2,1)}, f32[1280,1024]{1,0:T(8,128)}, bf16[1280,1024]{1,0:T(8,128)(2,1)}, bf16[1024,1280]{1,0:T(8,128)(2,1)}, bf16[1024,12...) custom-call(bf16[1,5,16,16,1024]{4,3,2,1,0:T(8,128)(2,1)} %g_hbm.1, s32[1]{0:T(128)} %bitcast.live_ref, ...), custom_call_target="tpu_custom_call" | custom-call | flops 2684354560 | bytes 28835840 | tf_op jit(solution)/shard_map/mid/pallas_call | solution.py:481
  73.8 230.5 %core.1 = (bf16[1,5,16,16,1024]{4,3,2,1,0:T(8,128)(2,1)}, bf16[1,5,16,16,1024]{4,3,2,1,0:T(8,128)(2,1)}, f32[8,1024]{1,0:T(8,128)}, f32[8,1024]{1,0:T(8,128)}, b...) custom-call(s32[1]{0:T(128)} %bitcast.live_ref, ...), custom_call_target="tpu_custom_call" | custom-call | flops 85563801600 | bytes 112197632 | tf_op jit(solution)/shard_map/core/pallas_call | solution.py:860
  304.4 0.0 copy-start.3
  304.4 0.0 copy-start.2
  304.4 0.9 slice.6
  305.3 0.8 slice.7
  306.1 1.6 collective-permute-start.1
  307.7 1.7 copy.21
  309.4 1.7 copy.22
  311.1 0.0 copy-start.1
  311.1 1.9 copy.23
  312.9 1.7 copy.24
  314.6 0.0 copy-done.3
  314.6 1.2 copy.25
  315.8 0.0 copy-done.2
  315.8 1.2 copy.26
  317.0 0.0 collective-permute-done.1
  317.0 0.6 copy.19
  317.6 0.0 copy-done.1
  317.6 0.0 copy-start
  317.6 1.5 copy.31
  319.1 1.2 copy-done
  320.3 1.5 copy.32
  (2 shorter events, 0.0 us)
Async XLA Ops:
  1.8 23.4 %collective-permute-start = (bf16[5,4,16,1024]{3,2,1,0:T(8,128)(2,1)S(1)}, bf16[5,4,16,1024]{3,2,1,0:T(8,128)(2,1)S(1)}, u32[]{:S(2)}, u32[]{:S(2)}) collective-permute-start(bf16[5,4,16,1024]{3,2,1,0:T(8,128)(2,1)S(1)} %dynamic-slice_bitcast_fusion), channel_id=1, source_target_pairs={{0,1},{1,0},{2,3},{3,2},{4,5},{5,4},{6,7},{7,6},{8,9},{9,8},{10,11... | collective-permute-start | bytes 1966088 | tf_op jit(solution)/shard_map/ppermute | solution.py:902
  25.2 0.8 copy-start.4
  304.4 10.3 %copy-start.3 = (f32[64,4096]{1,0:T(8,128)S(1)}, f32[64,4096]{1,0:T(8,128)}, u32[]{:S(2)}) copy-start(f32[64,4096]{1,0:T(8,128)} %get-tuple-element.59) | copy-start | bytes 3145732
  304.4 11.4 %copy-start.2 = (f32[4,64,1024]{2,1,0:T(8,128)S(1)}, f32[4,64,1024]{2,1,0:T(8,128)}, u32[]{:S(2)}) copy-start(f32[4,64,1024]{2,1,0:T(8,128)} %get-tuple-element.60) | copy-start | bytes 3145732
  306.1 10.9 %collective-permute-start.1 = (f32[6,1024]{1,0:T(8,128)S(1)}, f32[6,1024]{1,0:T(8,128)S(1)}, u32[]{:S(2)}, u32[]{:S(2)}) collective-permute-start(f32[6,1024]{1,0:T(8,128)S(1)} %pad_maximum_fusion), channel_id=1, source_target_pairs={{0,1},{1,0},{2,3},{3,2},{4,5},{5,4},{6,7},{7,6},{8,9},{9,8},{10,11... | collective-permute-start | bytes 73736 | tf_op jit(solution)/shard_map/ppermute | solution.py:902
  311.1 6.5 %copy-start.1 = (bf16[1,5,16,16,1024]{4,3,2,1,0:T(8,128)(2,1)S(1)}, bf16[1,5,16,16,1024]{4,3,2,1,0:T(8,128)(2,1)}, u32[]{:S(2)}) copy-start(bf16[1,5,16,16,1024]{4,3,2,1,0:T(8,128)(2,1)} %get-tuple-element.81) | copy-start | bytes 7864324
  317.6 2.7 copy-start
where the time goes:
time: 323 us; the launch traced here: 322 us
  Pallas kernels  294 us (91%)
  local copies, waits for them, and re-layouts  20.4 us (6%)
  starting transfers between devices  4.66 us (1%)
    pallas_call x1, Pallas kernels, core(): pl.pallas_call(functools.partial(core_kernel, til, plan, reds), grid=(pla...  231 us
    pallas_call x1, Pallas kernels, attn_fwd(): pl.pallas_call(attn_fwd_kernel, grid=(d // 128,), in_specs=[pl.BlockSpec(...  27.7 us
    pallas_call x2, Pallas kernels, pre(): pl.pallas_call(functools.partial(pre_kernel, n_group, from_spots), grid=(...  22.4 us
    unnamed x20, local copies, waits for them, and re-layouts  16.3 us
    pallas_call x1, Pallas kernels, mid(): pl.pallas_call(mid_kernel, grid=(5,), in_specs=[ANY, pl.BlockSpec(memory_...  13.3 us
  transfers between devices with their start and end apart: 2, of which 0 were waited for; matrix products, arithmetic and copies ran while one was open for 4% of the time, Pallas kernels for 5%

commit v1 on v0

--- a/solution.py
+++ b/solution.py
@@ -42,6 +42,17 @@
     return pl.BlockSpec(shape, lambda *_: (0,) * len(shape), pipeline_mode=pl.Buffered(1))
 
 
+def own_live(flags):
+    return jnp.where(flags[0, lax.axis_index("band")] == 1, 1.0, 0.0)
+
+
+def halo_bias(flags, shape, dim, r):
+    band = lax.axis_index("band")
+    other = jnp.where(flags[0, 1 - band] == 1, 0.0, MASKED)
+    off = jnp.where(flags[0, band] == 1, other, 0.0)
+    return jnp.where(lax.broadcasted_iota(jnp.int32, shape, dim) >= r, off, 0.0)
+
+
 def norm_stats(v):
     c = v - jnp.mean(v, axis=-1, keepdims=True)
     r = lax.rsqrt(jnp.mean(c * c, axis=-1, keepdims=True) + EPS)
@@ -57,73 +68,92 @@
     return pltpu.make_async_copy(there, vmem.at[s], sem.at[s])
 
 
-def pre_kernel(n_group, from_spots, x_hbm, mod_ref, *refs):
-    n_mat = (len(refs) - 5) // 2 if from_spots else (len(refs) - 3) // 2
-    w_refs = refs[:n_mat]
-    outs = refs[n_mat:]
-    if from_spots:
-        xw_ref, normed_ref = outs[:2]
-        o_refs = outs[2 : 2 + n_mat]
-    else:
-        o_refs = outs[:n_mat]
-    stage, sem, nsc = outs[-3:] if not from_spots else outs[-3:]
+def pre_kernel(
+    x_hbm, mod_ref, wq_ref, wk_ref, wv_ref, xw_ref, ndt_ref, q_ref, k_ref, v_ref, kh_ref, vh_ref,
+    stage, halo, sem, swap_sem, nsc, nhalo,
+):
+    step, n_tile = pl.program_id(0), pl.num_programs(0) // 2
+    band = lax.axis_index("band")
+    n_group = stage.shape[0]
     rows = nsc.shape[0] // n_group
-
-    @pl.when(pl.program_id(0) == 0)
-    def _():
-        band = lax.axis_index("band")
-        if from_spots:
-            copies = [spot_copy(x_hbm, stage, band, s, sem) for s in range(n_group)]
-        else:
-            copies = [
-                pltpu.make_async_copy(x_hbm.at[:, :, pl.ds(8 * s, 8), :], stage.at[s], sem.at[s])
-                for s in range(n_group)
-            ]
-        for c in copies:
-            c.start()
+    there = (lax.axis_index("dp"), 1 - band)
+
+    def normed(x):
+        n, _ = norm_stats(x)
+        return (n * (1.0 + mod_ref[1:2, :]) + mod_ref[0:1, :]).astype(BF16)
+
+    swap = pltpu.make_async_remote_copy(
+        src_ref=x_hbm.at[0, :, pl.ds(12 - 12 * band, 4)],
+        dst_ref=halo,
+        send_sem=swap_sem.at[0],
+        recv_sem=swap_sem.at[1],
+        device_id=there,
+        device_id_type=pl.DeviceIdType.MESH,
+    )
+
+    @pl.when(step == 0)
+    def _():
         for s in range(n_group):
-            copies[s].wait()
+            spot_copy(x_hbm, stage, band, s, sem).start()
+        entered = pltpu.get_barrier_semaphore()
+        pl.semaphore_signal(entered, inc=1, device_id=there, device_id_type=pl.DeviceIdType.MESH)
+        pl.semaphore_wait(entered, 1)
+        swap.start()
+        for s in range(n_group):
+            spot_copy(x_hbm, stage, band, s, sem).wait()
             x = stage[s].astype(F32).reshape(rows, stage.shape[-1])
-            n, _ = norm_stats(x)
-            part = pl.ds(s * rows, rows)
-            nsc[part, :] = (n * (1.0 + mod_ref[1:2, :]) + mod_ref[0:1, :]).astype(BF16)
-            if from_spots:
-                xw_ref[part, :] = x.astype(BF16)
-        if from_spots:
-            normed_ref[...] = jnp.transpose(nsc[...])
-
-    for w_ref, o_ref in zip(w_refs, o_refs):
-        o_ref[...] = dot(nsc[...], w_ref[...]).astype(BF16)
-
-
-def pre(x, mod, weights, n_group, from_spots):
-    d = x.shape[-1]
-    frames = x.shape[1] if from_spots else x.shape[0]
-    rows = frames * 32
-    t = n_group * rows
+            part = slice(s * rows, (s + 1) * rows)
+            nsc[part, :] = normed(x)
+            xw_ref[part, :] = x.astype(BF16)
+        ndt_ref[...] = jnp.transpose(nsc[...])
+
+    @pl.when(step < n_tile)
+    def _():
+        for w_ref, o_ref in ((wq_ref, q_ref), (wk_ref, k_ref), (wv_ref, v_ref)):
+            o_ref[...] = dot(nsc[...], w_ref[...]).astype(BF16)
+
+    @pl.when(step == n_tile)
+    def _():
+        swap.wait()
+        for j in range(2):
+            x = halo[:, :, 8 * j : 8 * j + 8, :].astype(F32).reshape(rows, halo.shape[-1])
+            nhalo[j * rows : (j + 1) * rows, :] = normed(x)
+
+    @pl.when(step >= n_tile)
+    def _():
+        for w_ref, o_ref in ((wk_ref, kh_ref), (wv_ref, vh_ref)):
+            o_ref[...] = dot(nhalo[...], w_ref[...]).astype(BF16)
+
+
+def pre(x, mod, wq, wk, wv):
+    d, frames = x.shape[-1], x.shape[1]
+    t = 8 * frames * 32
+    th = t // 4
     tile = 256
-    o_tile = pl.BlockSpec((t, tile), lambda n: (0, n))
-    full = pl.BlockSpec((t, d), lambda n: (0, 0))
-    act = jax.ShapeDtypeStruct((t, d), BF16)
-    k = len(weights)
-    head = [act, jax.ShapeDtypeStruct((d, t), BF16)] if from_spots else []
+    n_tile = d // tile
+    own = pl.BlockSpec((t, tile), lambda n: (0, jnp.minimum(n, n_tile - 1)))
+    other = pl.BlockSpec((th, tile), lambda n: (0, jnp.maximum(n - n_tile, 0)))
+    once = pl.BlockSpec((d, tile), lambda n: (0, jnp.minimum(n, n_tile - 1)))
+    twice = pl.BlockSpec((d, tile), lambda n: (0, lax.rem(n, n_tile)))
+    act, act_h = jax.ShapeDtypeStruct((t, d), BF16), jax.ShapeDtypeStruct((th, d), BF16)
     return pl.pallas_call(
-        functools.partial(pre_kernel, n_group, from_spots),
-        grid=(d // tile,),
-        in_specs=[ANY, whole((6, d))] + [pl.BlockSpec((d, tile), lambda n: (0, n))] * k,
-        out_specs=[full, whole((d, t))][: len(head)] + [o_tile] * k,
-        out_shape=head + [act] * k,
+        pre_kernel,
+        grid=(2 * n_tile,),
+        in_specs=[ANY, whole((6, d)), once, twice, twice],
+        out_specs=[whole((t, d)), whole((d, t)), own, own, own, other, other],
+        out_shape=[act, jax.ShapeDtypeStruct((d, t), BF16), act, act, act, act_h, act_h],
         scratch_shapes=[
-            pltpu.VMEM((n_group, frames, 4, 8, d), BF16),
-            pltpu.SemaphoreType.DMA((n_group,)),
+            pltpu.VMEM((8, frames, 4, 8, d), BF16),
+            pltpu.VMEM((frames, 4, 16, d), BF16),
+            pltpu.SemaphoreType.DMA((8,)),
+            pltpu.SemaphoreType.DMA((2,)),
             pltpu.VMEM((t, d), BF16),
+            pltpu.VMEM((th, d), BF16),
         ],
-        compiler_params=params(),
-        name="pre" if from_spots else "pre_halo",
-        cost_estimate=pl.CostEstimate(
-            flops=2 * t * d * d * k, bytes_accessed=2 * (k * d * d + (k + 3) * t * d), transcendentals=0
-        ),
-    )(x, mod, *weights)
+        compiler_params=params(collective_id=2, has_side_effects=True),
+        name="pre",
+        cost_estimate=pl.CostEstimate(flops=7 * t * d * d, bytes_accessed=10 * d * d + 12 * t * d, transcendentals=0),
+    )(x, mod, wq, wk, wv)
 
 
 LANES = 512
@@ -382,12 +412,11 @@
         scratch[2 * r * w + r : 2 * r * (w + 1), :] = halo_ref[r * w : r * (w + 1), :]
 
 
-def attn_fwd_kernel(ok_ref, q_ref, k_ref, v_ref, kh_ref, vh_ref, o_ref, lse_ref, kc, vc):
+def attn_fwd_kernel(live_ref, q_ref, k_ref, v_ref, kh_ref, vh_ref, o_ref, lse_ref, kc, vc):
     r = q_ref.shape[0] // 8
     fill_shared(kc, k_ref, kh_ref, r)
     fill_shared(vc, v_ref, vh_ref, r)
-    col = lax.broadcasted_iota(jnp.int32, (1, 2 * r), 1)
-    bias = jnp.where((col >= r) & (ok_ref[0] != 1), MASKED, 0.0)
+    bias = halo_bias(live_ref, (1, 2 * r), 1, r)
     for w, (q0, qn) in enumerate(((0, r), (r, r), (2 * r, 2 * r), (4 * r, 2 * r), (6 * r, r), (7 * r, r))):
         rows = slice(q0, q0 + qn)
         q = q_ref[rows, :]
@@ -417,7 +446,7 @@
     return pl.cdiv(t // 4, 128) * 128
 
 
-def attn_fwd(halo_ok, q, k, v, kh, vh):
+def attn_fwd(live, q, k, v, kh, vh):
     t, d = q.shape
     th = kh.shape[0]
     big = pl.BlockSpec((t, 128), lambda n: (0, n))
@@ -432,7 +461,7 @@
         compiler_params=params(),
         name="attn_fwd",
         cost_estimate=pl.CostEstimate(flops=t * t * d, bytes_accessed=12 * t * d, transcendentals=t * t * 3),
-    )(halo_ok, q, k, v, kh, vh)
+    )(live, q, k, v, kh, vh)
 
 
 def mid_kernel(
@@ -440,7 +469,7 @@
 ):
     step = pl.program_id(0)
     band = lax.axis_index("band")
-    live = live_ref[0].astype(F32)
+    live = own_live(live_ref)
     n_group = stage.shape[0]
     rows = gw_ref.shape[0] // n_group
 
@@ -607,11 +636,11 @@
 
 
 def core_kernel(
-    til, plan, reds, live_ref, ok_ref, nm_hbm, gm_hbm, nmt_hbm, attt_hbm, ndt_hbm, wu_hbm, wo_hbm, wq_hbm,
+    til, plan, reds, live_ref, nm_hbm, gm_hbm, nmt_hbm, attt_hbm, ndt_hbm, wu_hbm, wo_hbm, wq_hbm,
     wd_ref, mid_ref, g_ref, ao_ref, mod_ref, wk_ref, wv_ref, q_ref, k_ref, v_ref, lse_ref, kh_ref, vh_ref, x_ref,
-    out_hbm, gin_hbm, sums_ref, sums_a_ref, dwd_hbm, gup_hbm, gdown_hbm, gout_hbm, gq_hbm, gk_hbm, gv_hbm,
+    out_hbm, gin_hbm, sums_ref, dwd_hbm, gup_hbm, gdown_hbm, gout_hbm, gq_hbm, gk_hbm, gv_hbm,
     buf_a, buf_b, buf_c, buf_t, mo, h, do_s, w0, wu, dwd, tiles, kc, vc, own, hsend, hrecv,
-    hsem, wsem, lsem, stage, sem, *scratch,
+    hsem, wsem, lsem, stage, sem, sums_m, sums_a, sums_got, *scratch,
 ):
     step, steps = pl.program_id(0), pl.num_programs(0)
     n_ff, n_att, width = plan.n_ff, plan.n_att, til.width
@@ -729,7 +758,7 @@
                 store_down(step - 1, k).wait()
 
         part = pl.ds(pl.multiple_of(block * chunk, chunk), chunk)
-        live = live_ref[0].astype(F32)
+        live = own_live(live_ref)
         middle, g = mid_ref[...], g_ref[...].astype(F32)
         mlp_out, hh = mo[part, :], h[part, :]
         n, rs = norm_stats(middle)
@@ -739,7 +768,7 @@
         buf_b[part, :] = ga
         do_s[part, :] = dot(ga, w0[...], 1, 1).astype(BF16)
         sums = [col_sum(live * ao_ref[...].astype(F32) * gmid), col_sum(hh), col_sum(hh * n), col_sum(live * mlp_out * g)]
-        add_sums(sums_ref, block == 0, sums)
+        add_sums(sums_m, block == 0, sums)
         put_groups(middle + (live * mod_ref[5:6, :]) * mlp_out, stage, out_hbm, sem, block, 4)
 
     @pl.when(step == plan.out)
@@ -776,8 +805,7 @@
         lanes = pl.ds(pl.multiple_of(now * 128, 128), 128)
         fill_shared(kc, k_ref, kh_ref, r)
         fill_shared(vc, v_ref, vh_ref, r)
-        row = lax.broadcasted_iota(jnp.int32, (2 * r, 1), 0)
-        bias = jnp.where((row >= r) & (ok_ref[0] != 1), MASKED, 0.0)
+        bias = halo_bias(live_ref, (2 * r, 1), 0, r)
 
         def window(w, i, rows, keys, shared):
             data = (bias, q_ref, kc, vc) if shared else (None, q_ref, k_ref, v_ref)
@@ -808,15 +836,21 @@
             one.tick(plan.fin + 2 * i + 1)
         hh = hh + dot(buf_c[part, :], wv_ref[...], 1, 1)
         n, rs = norm_stats(x_ref[...].astype(F32))
-        add_sums(sums_a_ref, i == 0, [col_sum(hh), col_sum(hh * n)])
+        add_sums(sums_a, i == 0, [col_sum(hh), col_sum(hh * n)])
         put_groups(h[part, :] + norm_back(hh, n, rs, mod_ref[1:2, :]), stage, gin_hbm, sem, i, 4)
 
     @pl.when(step == steps - 1)
     def _():
+        rows = [sums_a[0:2, :], sums_m[0:4, :], jnp.zeros((2, d), F32)]
+        sums_a[...] = jnp.concatenate(rows, axis=0)
+        other = red.plain(sums_a, sums_got, hsem.at[3], hsem.at[4], 0)
+        other.start()
         finish(reds, plan.end)
-
-
-def core(live, halo_ok, nm, gm, nmt, attt, ndt, w_up, w_down, wo, wq, wk, wv, middle, gw, ao, mod, q, k, v, lse, kh, vh, xw, like):
+        other.wait()
+        sums_ref[...] = sums_a[...] + sums_got[...]
+
+
+def core(live, nm, gm, nmt, attt, ndt, w_up, w_down, wo, wq, wk, wv, middle, gw, ao, mod, q, k, v, lse, kh, vh, xw, like):
     t, d = nm.shape
     ff = w_up.shape[1]
     th = kh.shape[0]
@@ -860,10 +894,10 @@
     return pl.pallas_call(
         functools.partial(core_kernel, til, plan, reds),
         grid=(plan.steps,),
-        in_specs=[smem, smem] + [ANY] * 8 + [down, post, post, post, whole((6, d)), whole((d, d)), whole((d, d))]
+        in_specs=[smem] + [ANY] * 8 + [down, post, post, post, whole((6, d)), whole((d, d)), whole((d, d))]
         + [big] * 3 + [lse_spec] + [small] * 2 + [last],
-        out_specs=[ANY, ANY, full, full] + [ANY] * 7,
-        out_shape=[image, image, sums, sums, jax.ShapeDtypeStruct(cube, BF16), jax.ShapeDtypeStruct((red.r, ff), F32)]
+        out_specs=[ANY, ANY, full] + [ANY] * 7,
+        out_shape=[image, image, sums, jax.ShapeDtypeStruct(cube, BF16), jax.ShapeDtypeStruct((red.r, ff), F32)]
         + [jax.ShapeDtypeStruct((ff // d, red.r, d), F32), share, share, share, share],
         scratch_shapes=[
             act,
@@ -882,12 +916,13 @@
             pltpu.VMEM((2, th, 128), F32),
             pltpu.VMEM((2, th, 128), BF16),
             pltpu.VMEM((2, 2, th, 128), BF16),
-            pltpu.SemaphoreType.DMA((3,)),
+            pltpu.SemaphoreType.DMA((5,)),
             pltpu.SemaphoreType.DMA((3, PIECES)),
             pltpu.SemaphoreType.DMA((7,)),
             pltpu.VMEM((4, frames, 4, 8, d), BF16),
             pltpu.SemaphoreType.DMA((4,)),
         ]
+        + [pltpu.VMEM((8, d), F32)] * 3
         + reds[0].scratch()
         + reds[1].scratch(),
         compiler_params=params(limit=63 * 1024 * 1024, collective_id=1, has_side_effects=True),
@@ -895,39 +930,67 @@
         cost_estimate=pl.CostEstimate(
             flops=12 * t * d * (ff + d) + 3 * t * t * d, bytes_accessed=8 * d * ff + 60 * t * d, transcendentals=t * (ff + 3 * t)
         ),
-    )(live, halo_ok, nm, gm, nmt, attt, ndt, w_up, wo, wq, w_down, middle, gw, ao, mod, wk, wv, q, k, v, lse, kh, vh, xw)
-
-
-def band_swap(v):
-    return lax.ppermute(v, "band", [(0, 1), (1, 0)])
+    )(live, nm, gm, nmt, attt, ndt, w_up, wo, wq, w_down, middle, gw, ao, mod, wk, wv, q, k, v, lse, kh, vh, xw)
+
+
+def results_kernel(n_grad, a_hbm, b_hbm, mod_ref, *refs):
+    grads, (a_out, b_out, mod_out), flats = refs[:n_grad], refs[n_grad : n_grad + 3], refs[n_grad + 3 : 2 * n_grad + 3]
+    held, sem = refs[-2:]
+    loads, stores = [], []
+    for n, (src, dst) in enumerate(((a_hbm, a_out), (b_hbm, b_out))):
+        for f in range(src.shape[1]):
+            loads.append(pltpu.make_async_copy(src.at[0, f], held.at[n, f], sem.at[0, n, f]))
+            stores.append(pltpu.make_async_copy(held.at[n, f], dst.at[0, f], sem.at[1, n, f]))
+    for c in loads:
+        c.start()
+    mod_out[0] = mod_ref[0:6, :]
+    for src, dst in zip(grads, flats):
+        rows, cols = src.shape
+        wide = cols // 128
+        for g in range(wide):
+            dst[pl.ds(g, rows, stride=wide), :] = src[:, lanes_at(g, 128)]
+    for load, store in zip(loads, stores):
+        load.wait()
+        store.start()
+    for c in stores:
+        c.wait()
+
+
+def results(image_a, image_b, mod_sums, grads):
+    grads = [g.reshape(-1, g.shape[-1]) for g in grads]
+    vmem = pl.BlockSpec(memory_space=pltpu.VMEM)
+    n = len(grads)
+    out = pl.pallas_call(
+        functools.partial(results_kernel, n),
+        in_specs=[ANY, ANY] + [vmem] * (n + 1),
+        out_specs=[ANY, ANY] + [vmem] * (n + 1),
+        out_shape=[jax.ShapeDtypeStruct(image_a.shape, BF16)] * 2
+        + [jax.ShapeDtypeStruct((1, 6, mod_sums.shape[1]), F32)]
+        + [jax.ShapeDtypeStruct((g.size // 128, 128), F32) for g in grads],
+        scratch_shapes=[
+            pltpu.VMEM((2,) + image_a.shape[1:], BF16),
+            pltpu.SemaphoreType.DMA((2, 2, image_a.shape[1])),
+        ],
+        compiler_params=params(),
+        name="results",
+        cost_estimate=pl.CostEstimate(flops=0, bytes_accessed=8 * image_a.size, transcendentals=0),
+    )(image_a, image_b, mod_sums, *grads)
+    return out[0], out[1], out[2], *(g.reshape(-1) for g in out[3:])
 
 
 def on_device(
     block_input, modulation, band_live, w_query, w_key, w_value, w_out, w_up, w_down, cotangent
 ):
     assert lax.axis_size("band") == 2 and block_input.shape[2:4] == (16, 16)
-    band = lax.axis_index("band")
-    flags = band_live[0]
-    live_own = lax.dynamic_index_in_dim(flags, band, keepdims=True)
-    live_other = lax.dynamic_index_in_dim(flags, 1 - band, keepdims=True)
-    live = (live_own == 1).astype(jnp.int32)
-    halo_ok = ((live_other == 1) | (live_own != 1)).astype(jnp.int32)
     mod = modulation[0]
-
-    edge = lax.dynamic_slice_in_dim(block_input[0], 12 - 12 * band, 4, axis=1)
-    x_halo = band_swap(edge)
-    xw, ndt, q, k, v = pre(block_input, mod, (w_query, w_key, w_value), 8, True)
-    kh, vh = pre(x_halo, mod, (w_key, w_value), 2, False)
-    attended, lse = attn_fwd(halo_ok, q, k, v, kh, vh)
-    ao, middle, nm, nmt, attt, gw, gm = mid(cotangent, live, attended, w_out, xw, mod)
-    block_output, grad_input, sums_m, sums_a, _, g_up, g_down, g_out, g_query, g_key, g_value = core(
-        live, halo_ok, nm, gm, nmt, attt, ndt, w_up, w_down, w_out, w_query, w_key, w_value,
+    xw, ndt, q, k, v, kh, vh = pre(block_input, mod, w_query, w_key, w_value)
+    attended, lse = attn_fwd(band_live, q, k, v, kh, vh)
+    ao, middle, nm, nmt, attt, gw, gm = mid(cotangent, band_live, attended, w_out, xw, mod)
+    block_output, grad_input, mod_sums, _, g_up, g_down, g_out, g_query, g_key, g_value = core(
+        band_live, nm, gm, nmt, attt, ndt, w_up, w_down, w_out, w_query, w_key, w_value,
         middle, gw, ao, mod, q, k, v, lse, kh, vh, xw, block_input,
     )
-    mod_part = jnp.concatenate([sums_a[0:2], sums_m[0:4]])
-    mod_total = mod_part + band_swap(mod_part)
-    grads = (g_query, g_key, g_value, g_out, g_up, g_down)
-    return block_output, grad_input, mod_total[None], *(g.reshape(-1) for g in grads)
+    return results(block_output, grad_input, mod_sums, (g_query, g_key, g_value, g_out, g_up, g_down))
 
 
 def solution(mesh):

time: 323 us -> 314 us (0.972)
  local copies, waits for them, and re-layouts: 20.4 us -> 2.75 us
  Pallas kernels: 294 us -> 310 us
  starting transfers between devices: 4.66 us -> 0 us
    unnamed x20 -> x2, local copies, waits for them, and re-layouts: 16.3 us -> 2.75 us
    pallas_call x2, Pallas kernels: 22.4 us -> 33.7 us  [the longest x1 26.1 us: pre(): pl.pallas_call(pre_kernel, grid=(2 * n_tile,), in_specs=[ANY, whole((6, d...]
    ppermute x2 -> x0, starting transfers between devices: 4.66 us -> none  [band_swap(): return lax.ppermute(v, 'band', [(0, 1), (1, 0)])]
    pallas_call x1, Pallas kernels: 231 us -> 234 us  [core(): pl.pallas_call(functools.partial(core_kernel, til, plan, reds), grid=(pla...]
  transfers between devices with their start and end apart: 2 -> 0, of which waited for: 0 -> 0; matrix products, arithmetic and copies ran while one was open for 4% -> 0% of each run, Pallas kernels for 5% -> 0%
where the time goes in v1:
time: 314 us; the launch traced here: 313 us
  Pallas kernels  310 us (99%)
    pallas_call x1, Pallas kernels, core(): pl.pallas_call(functools.partial(core_kernel, til, plan, reds), grid=(pla...  234 us
    pallas_call x1, Pallas kernels, attn_fwd(): pl.pallas_call(attn_fwd_kernel, grid=(d // 128,), in_specs=[pl.BlockSpec(...  27.8 us
    pallas_call x1, Pallas kernels, pre(): pl.pallas_call(pre_kernel, grid=(2 * n_tile,), in_specs=[ANY, whole((6, d...  26.1 us
    pallas_call x1, Pallas kernels, mid(): pl.pallas_call(mid_kernel, grid=(5,), in_specs=[ANY, pl.BlockSpec(memory_...  13.6 us
    pallas_call x1, Pallas kernels, results(): pl.pallas_call(functools.partial(results_kernel, n), in_specs=[ANY, ANY]...  7.61 us

profile of v1, /device:TPU:0, one launch (start us, length us, event | category | flops | bytes accessed | tf_op | source)
XLA Modules:
  0.0 313.0 jit_solution(13187559144158053797)
XLA Ops:
  0.6 1.4 copy.22
  2.0 26.1 %pre.1 = (bf16[1280,1024]{1,0:T(8,128)(2,1)}, bf16[1024,1280]{1,0:T(8,128)(2,1)}, bf16[1280,1024]{1,0:T(8,128)(2,1)}, bf16[1280,1024]{1,0:T(8,128)(2,1)}, bf16[1...) custom-call(bf16[1,5,16,16,1024]{4,3,2,1,0:T(8,128)(2,1)} %x_hbm.1, ...), custom_call_target="tpu_custom_call" | custom-call | flops 9395240960 | bytes 26214400 | tf_op jit(solution)/shard_map/pre/pallas_call | solution.py:139
  28.1 27.8 %attn_fwd.1 = (bf16[1280,1024]{1,0:T(8,128)(2,1)}, f32[8,6,8,384]{3,2,1,0:T(8,128)}) custom-call(s32[1,2]{1,0:T(1,128)} %live_ref.5, bf16[1280,1024]{1,0:T(8,128)(2,1)} %get-tuple-element.43.q_ref, bf16[1280,1024]{1,0:T(8,128)(2,1)} %get-tuple-element.44.k_ref, bf16[1280,1024]{1,0:T(8,128)(2,1)} %get-tuple-element.45.v_ref, ...), custom_call_target="tpu_custom_call" | custom-call | flops 1677721600 | bytes 15728640 | tf_op jit(solution)/shard_map/attn_fwd/pallas_call | solution.py:454
  55.9 13.6 %mid.1 = (bf16[1280,1024]{1,0:T(8,128)(2,1)}, f32[1280,1024]{1,0:T(8,128)}, bf16[1280,1024]{1,0:T(8,128)(2,1)}, bf16[1024,1280]{1,0:T(8,128)(2,1)}, bf16[1024,12...) custom-call(bf16[1,5,16,16,1024]{4,3,2,1,0:T(8,128)(2,1)} %g_hbm.1, s32[1,2]{1,0:T(1,128)} %live_ref.5, ...), custom_call_target="tpu_custom_call" | custom-call | flops 2684354560 | bytes 28835840 | tf_op jit(solution)/shard_map/mid/pallas_call | solution.py:510
  69.5 234.5 %core.1 = (bf16[1,5,16,16,1024]{4,3,2,1,0:T(8,128)(2,1)}, bf16[1,5,16,16,1024]{4,3,2,1,0:T(8,128)(2,1)}, f32[8,1024]{1,0:T(8,128)}, bf16[8,2,4,64,1024]{4,3,2,1,...) custom-call(s32[1,2]{1,0:T(1,128)} %live_ref.5, ...), custom_call_target="tpu_custom_call" | custom-call | flops 85563801600 | bytes 112197632 | tf_op jit(solution)/shard_map/core/pallas_call | solution.py:894
  303.9 7.6 %results.1 = (bf16[1,5,16,16,1024]{4,3,2,1,0:T(8,128)(2,1)}, bf16[1,5,16,16,1024]{4,3,2,1,0:T(8,128)(2,1)}, f32[1,6,1024]{2,1,0:T(8,128)}, f32[512,128]{1,0:T(8,...) custom-call(bf16[1,5,16,16,1024]{4,3,2,1,0:T(8,128)(2,1)} %get-tuple, ...), custom_call_target="tpu_custom_call" | custom-call | bytes 10485760 | tf_op jit(solution)/shard_map/results/pallas_call | solution.py:963
  311.6 1.4 copy.19

commit v2 on v1

--- a/solution.py
+++ b/solution.py
@@ -69,7 +69,8 @@
 
 
 def pre_kernel(
-    x_hbm, mod_ref, wq_ref, wk_ref, wv_ref, xw_ref, ndt_ref, q_ref, k_ref, v_ref, kh_ref, vh_ref,
+    x_hbm, g_hbm, live_ref, mod_ref, wq_ref, wk_ref, wv_ref,
+    xw_ref, ndt_ref, gw_ref, gm_ref, q_ref, k_ref, v_ref, kh_ref, vh_ref,
     stage, halo, sem, swap_sem, nsc, nhalo,
 ):
     step, n_tile = pl.program_id(0), pl.num_programs(0) // 2
@@ -105,7 +106,8 @@
             part = slice(s * rows, (s + 1) * rows)
             nsc[part, :] = normed(x)
             xw_ref[part, :] = x.astype(BF16)
-        ndt_ref[...] = jnp.transpose(nsc[...])
+        for s in range(n_group):
+            spot_copy(g_hbm, stage, band, s, sem).start()
 
     @pl.when(step < n_tile)
     def _():
@@ -114,6 +116,14 @@
 
     @pl.when(step == n_tile)
     def _():
+        ndt_ref[...] = jnp.transpose(nsc[...])
+        gate = own_live(live_ref) * mod_ref[5:6, :]
+        for s in range(n_group):
+            spot_copy(g_hbm, stage, band, s, sem).wait()
+            g = stage[s].astype(F32).reshape(rows, stage.shape[-1])
+            part = slice(s * rows, (s + 1) * rows)
+            gw_ref[part, :] = g.astype(BF16)
+            gm_ref[part, :] = (gate * g).astype(BF16)
         swap.wait()
         for j in range(2):
             x = halo[:, :, 8 * j : 8 * j + 8, :].astype(F32).reshape(rows, halo.shape[-1])
@@ -125,7 +135,7 @@
             o_ref[...] = dot(nhalo[...], w_ref[...]).astype(BF16)
 
 
-def pre(x, mod, wq, wk, wv):
+def pre(x, cot, live, mod, wq, wk, wv):
     d, frames = x.shape[-1], x.shape[1]
     t = 8 * frames * 32
     th = t // 4
@@ -139,9 +149,9 @@
     return pl.pallas_call(
         pre_kernel,
         grid=(2 * n_tile,),
-        in_specs=[ANY, whole((6, d)), once, twice, twice],
-        out_specs=[whole((t, d)), whole((d, t)), own, own, own, other, other],
-        out_shape=[act, jax.ShapeDtypeStruct((d, t), BF16), act, act, act, act_h, act_h],
+        in_specs=[ANY, ANY, pl.BlockSpec(memory_space=pltpu.SMEM), whole((6, d)), once, twice, twice],
+        out_specs=[whole((t, d)), whole((d, t)), whole((t, d)), whole((t, d)), own, own, own, other, other],
+        out_shape=[act, jax.ShapeDtypeStruct((d, t), BF16), act, act, act, act, act, act_h, act_h],
         scratch_shapes=[
             pltpu.VMEM((8, frames, 4, 8, d), BF16),
             pltpu.VMEM((frames, 4, 16, d), BF16),
@@ -153,7 +163,7 @@
         compiler_params=params(collective_id=2, has_side_effects=True),
         name="pre",
         cost_estimate=pl.CostEstimate(flops=7 * t * d * d, bytes_accessed=10 * d * d + 12 * t * d, transcendentals=0),
-    )(x, mod, wq, wk, wv)
+    )(x, cot, live, mod, wq, wk, wv)
 
 
 LANES = 512
@@ -398,12 +408,13 @@
 
 def window_pair(r, first, rows, at, shared, body):
     def one(i, _):
-        q0 = pl.multiple_of(at + i * rows, 32)
-        k0 = pl.multiple_of(2 * r * i, 32) if shared else q0
+        q0 = at + i * rows
+        k0 = 2 * r * i if shared else q0
         body(first + i, i, pl.ds(q0, rows), pl.ds(k0, 2 * r if shared else rows), shared)
         return 0
 
-    lax.fori_loop(0, 2, one, 0)
+    for i in range(2):
+        one(i, 0)
 
 
 def fill_shared(scratch, own_ref, halo_ref, r):
@@ -464,20 +475,8 @@
     )(live, q, k, v, kh, vh)
 
 
-def mid_kernel(
-    g_hbm, live_ref, att_ref, w_ref, x_ref, mod_ref, ao_ref, mid_ref, nm_ref, nmt_ref, attt_ref, gw_ref, gm_ref, stage, sem
-):
-    step = pl.program_id(0)
-    band = lax.axis_index("band")
+def mid_kernel(live_ref, att_ref, w_ref, x_ref, mod_ref, ao_ref, mid_ref, nm_ref, nmt_ref, attt_ref):
     live = own_live(live_ref)
-    n_group = stage.shape[0]
-    rows = gw_ref.shape[0] // n_group
-
-    @pl.when(step == 0)
-    def _():
-        for s in range(n_group):
-            spot_copy(g_hbm, stage, band, s, sem).start()
-
     attn_out = dot(att_ref[...], w_ref[...])
     middle = x_ref[...].astype(F32) + (live * mod_ref[2:3, :]) * attn_out
     ao_ref[...] = attn_out.astype(BF16)
@@ -487,37 +486,24 @@
     nm_ref[...] = nm
     nmt_ref[...] = jnp.transpose(nm)
     attt_ref[...] = jnp.transpose(att_ref[...])
-    for k in range(4):
-
-        @pl.when(step == k + 1)
-        def _():
-            for s in range(2 * k, 2 * k + 2):
-                spot_copy(g_hbm, stage, band, s, sem).wait()
-                g = stage[s].astype(F32).reshape(rows, stage.shape[-1])
-                part = slice(s * rows, (s + 1) * rows)
-                gw_ref[part, :] = g.astype(BF16)
-                gm_ref[part, :] = ((live * mod_ref[5:6, :]) * g).astype(BF16)
-
-
-def mid(cot, live, attended, w_out, xw, mod):
+
+
+def mid(live, attended, w_out, xw, mod):
     t, d = xw.shape
-    frames = cot.shape[1]
     blk = pl.BlockSpec((t // 5, d), lambda m: (m, 0))
     blk_t = pl.BlockSpec((d, t // 5), lambda m: (0, m))
-    full = pl.BlockSpec((t, d), lambda m: (0, 0))
     bf, f32 = jax.ShapeDtypeStruct((t, d), BF16), jax.ShapeDtypeStruct((t, d), F32)
     bf_t = jax.ShapeDtypeStruct((d, t), BF16)
     return pl.pallas_call(
         mid_kernel,
         grid=(5,),
-        in_specs=[ANY, pl.BlockSpec(memory_space=pltpu.SMEM), blk, whole((d, d)), blk, whole((6, d))],
-        out_specs=[blk, blk, blk, blk_t, blk_t, full, full],
-        out_shape=[bf, f32, bf, bf_t, bf_t, bf, bf],
-        scratch_shapes=[pltpu.VMEM((8, frames, 4, 8, d), BF16), pltpu.SemaphoreType.DMA((8,))],
+        in_specs=[pl.BlockSpec(memory_space=pltpu.SMEM), blk, whole((d, d)), blk, whole((6, d))],
+        out_specs=[blk, blk, blk, blk_t, blk_t],
+        out_shape=[bf, f32, bf, bf_t, bf_t],
         compiler_params=params(),
         name="mid",
-        cost_estimate=pl.CostEstimate(flops=2 * t * d * d, bytes_accessed=22 * t * d, transcendentals=0),
-    )(cot, live, attended, w_out, xw, mod)
+        cost_estimate=pl.CostEstimate(flops=2 * t * d * d, bytes_accessed=16 * t * d, transcendentals=0),
+    )(live, attended, w_out, xw, mod)
 
 
 GELU_C = 0.7978845608
@@ -718,7 +704,7 @@
         up = wu.at[slot]
 
         def rows(i, _):
-            part = pl.ds(pl.multiple_of(i * chunk, chunk), chunk)
+            part = pl.ds(pl.multiple_of(i * (2 * chunk), 2 * chunk), 2 * chunk)
             v = dot(buf_b[part, :], up[...])
             gh = dot(buf_c[part, :], wd, 1, 1)
             v2 = v * v
@@ -733,7 +719,7 @@
             h[part, :] += dot(gpre, up[...], 1, 1)
             return 0
 
-        lax.fori_loop(0, 4, rows, 0)
+        lax.fori_loop(0, 2, rows, 0)
 
         @pl.when(step > 0)
         def _():
@@ -812,7 +798,7 @@
             dq, dk, dv = window_back(w, rows, keys, *data, do_s[rows, lanes], lse_ref)
             buf_a[rows, lanes] = dq.astype(BF16)
             if shared:
-                part = pl.ds(pl.multiple_of(i * r, 32), r)
+                part = pl.ds(i * r, r)
                 for n, v in enumerate((dk, dv)):
                     own[n, part, :] = v[:r, :]
                     hsend[n, part, :] = v[r:, :].astype(BF16)
@@ -983,9 +969,9 @@
 ):
     assert lax.axis_size("band") == 2 and block_input.shape[2:4] == (16, 16)
     mod = modulation[0]
-    xw, ndt, q, k, v, kh, vh = pre(block_input, mod, w_query, w_key, w_value)
+    xw, ndt, gw, gm, q, k, v, kh, vh = pre(block_input, cotangent, band_live, mod, w_query, w_key, w_value)
     attended, lse = attn_fwd(band_live, q, k, v, kh, vh)
-    ao, middle, nm, nmt, attt, gw, gm = mid(cotangent, band_live, attended, w_out, xw, mod)
+    ao, middle, nm, nmt, attt = mid(band_live, attended, w_out, xw, mod)
     block_output, grad_input, mod_sums, _, g_up, g_down, g_out, g_query, g_key, g_value = core(
         band_live, nm, gm, nmt, attt, ndt, w_up, w_down, w_out, w_query, w_key, w_value,
         middle, gw, ao, mod, q, k, v, lse, kh, vh, xw, block_input,

time: 314 us -> 305 us (0.971)
  Pallas kernels: 310 us -> 301 us
    pallas_call x1, Pallas kernels: 234 us -> 227 us  [core(): pl.pallas_call(functools.partial(core_kernel, til, plan, reds), grid=(pla...]
where the time goes in v2:
time: 305 us; the launch traced here: 304 us
  Pallas kernels  301 us (99%)
    pallas_call x1, Pallas kernels, core(): pl.pallas_call(functools.partial(core_kernel, til, plan, reds), grid=(pla...  227 us
    pallas_call x1, Pallas kernels, pre(): pl.pallas_call(pre_kernel, grid=(2 * n_tile,), in_specs=[ANY, ANY, pl.Blo...  27.8 us
    pallas_call x1, Pallas kernels, attn_fwd(): pl.pallas_call(attn_fwd_kernel, grid=(d // 128,), in_specs=[pl.BlockSpec(...  27.8 us
    pallas_call x1, Pallas kernels, mid(): pl.pallas_call(mid_kernel, grid=(5,), in_specs=[pl.BlockSpec(memory_space...  10.7 us
    pallas_call x1, Pallas kernels, results(): pl.pallas_call(functools.partial(results_kernel, n), in_specs=[ANY, ANY]...  7.61 us

profile of v2, /device:TPU:0, one launch (start us, length us, event | category | flops | bytes accessed | tf_op | source)
XLA Modules:
  0.0 304.2 jit_solution(6029931181965646418)
XLA Ops:
  0.6 1.4 copy.22
  2.0 27.8 %pre.1 = (bf16[1280,1024]{1,0:T(8,128)(2,1)}, bf16[1024,1280]{1,0:T(8,128)(2,1)}, bf16[1280,1024]{1,0:T(8,128)(2,1)}, bf16[1280,1024]{1,0:T(8,128)(2,1)}, bf16[1...) custom-call(bf16[1,5,16,16,1024]{4,3,2,1,0:T(8,128)(2,1)} %x_hbm.1, ...), custom_call_target="tpu_custom_call" | custom-call | flops 9395240960 | bytes 26214400 | tf_op jit(solution)/shard_map/pre/pallas_call | solution.py:149
  29.8 27.8 %attn_fwd.1 = (bf16[1280,1024]{1,0:T(8,128)(2,1)}, f32[8,6,8,384]{3,2,1,0:T(8,128)}) custom-call(s32[1,2]{1,0:T(1,128)} %live_ref.7, bf16[1280,1024]{1,0:T(8,128)(2,1)} %get-tuple-element.43.q_ref, bf16[1280,1024]{1,0:T(8,128)(2,1)} %get-tuple-element.44.k_ref, bf16[1280,1024]{1,0:T(8,128)(2,1)} %get-tuple-element.45.v_ref, ...), custom_call_target="tpu_custom_call" | custom-call | flops 1677721600 | bytes 15728640 | tf_op jit(solution)/shard_map/attn_fwd/pallas_call | solution.py:465
  57.6 10.7 %mid.1 = (bf16[1280,1024]{1,0:T(8,128)(2,1)}, f32[1280,1024]{1,0:T(8,128)}, bf16[1280,1024]{1,0:T(8,128)(2,1)}, bf16[1024,1280]{1,0:T(8,128)(2,1)}, bf16[1024,1280]{1,0:T(8,128)(2,1)}) custom-call(s32[1,2]{1,0:T(1,128)} %live_ref.7, bf16[1280,1024]{1,0:T(8,128)(2,1)} %get-tuple-element.48.att_ref, bf16[1024,1024]{1,0:T(8,128)(2,1)} %wo_hbm.1, ...), custom_call_target="tpu_custom_call" | custom-call | flops 2684354560 | bytes 20971520 | tf_op jit(solution)/shard_map/mid/pallas_call | solution.py:497
  68.3 226.9 %core.1 = (bf16[1,5,16,16,1024]{4,3,2,1,0:T(8,128)(2,1)}, bf16[1,5,16,16,1024]{4,3,2,1,0:T(8,128)(2,1)}, f32[8,1024]{1,0:T(8,128)}, bf16[8,2,4,64,1024]{4,3,2,1,...) custom-call(s32[1,2]{1,0:T(1,128)} %live_ref.7, ...), custom_call_target="tpu_custom_call" | custom-call | flops 85563801600 | bytes 112197632 | tf_op jit(solution)/shard_map/core/pallas_call | solution.py:880
  295.2 7.6 %results.1 = (bf16[1,5,16,16,1024]{4,3,2,1,0:T(8,128)(2,1)}, bf16[1,5,16,16,1024]{4,3,2,1,0:T(8,128)(2,1)}, f32[1,6,1024]{2,1,0:T(8,128)}, f32[512,128]{1,0:T(8,...) custom-call(bf16[1,5,16,16,1024]{4,3,2,1,0:T(8,128)(2,1)} %get-tuple, ...), custom_call_target="tpu_custom_call" | custom-call | bytes 10485760 | tf_op jit(solution)/shard_map/results/pallas_call | solution.py:949
  302.8 1.4 copy.19

commit v3 on v2

--- a/solution.py
+++ b/solution.py
@@ -846,7 +846,10 @@
     n_ff, n_att = til.steps, d // 128
     plan = Plan(n_ff, n_att, til.early)
     rest = tuple(range(3, dp.bit_length() - 1))
-    reds = [Reduce(dp, d, ((0, 1, 2, *rest), (1, 2, 0, *rest)), i == 0) for i in range(2)]
+    reds = [
+        Reduce(dp, d, ((0, 1, 2, *rest), (1, 2, 0, *rest)), True),
+        Reduce(dp, d, ((1, 2, 0, *rest), (2, 1, 0, *rest)), False),
+    ]
     red = reds[0]
 
     def block_at(first, count):

time: 305 us -> 303 us (level)
  no operation moved by 1% of the time
where the time goes in v3:
time: 303 us; the launch traced here: 302 us
  Pallas kernels  299 us (99%)
    pallas_call x1, Pallas kernels, core(): pl.pallas_call(functools.partial(core_kernel, til, plan, reds), grid=(pla...  225 us
    pallas_call x1, Pallas kernels, pre(): pl.pallas_call(pre_kernel, grid=(2 * n_tile,), in_specs=[ANY, ANY, pl.Blo...  27.8 us
    pallas_call x1, Pallas kernels, attn_fwd(): pl.pallas_call(attn_fwd_kernel, grid=(d // 128,), in_specs=[pl.BlockSpec(...  27.8 us
    pallas_call x1, Pallas kernels, mid(): pl.pallas_call(mid_kernel, grid=(5,), in_specs=[pl.BlockSpec(memory_space...  10.7 us
    pallas_call x1, Pallas kernels, results(): pl.pallas_call(functools.partial(results_kernel, n), in_specs=[ANY, ANY]...  7.61 us

profile of v3, /device:TPU:0, one launch (start us, length us, event | category | flops | bytes accessed | tf_op | source)
XLA Modules:
  0.0 302.3 jit_solution(11474707170288850070)
XLA Ops:
  0.6 1.4 copy.22
  2.0 27.8 %pre.1 = (bf16[1280,1024]{1,0:T(8,128)(2,1)}, bf16[1024,1280]{1,0:T(8,128)(2,1)}, bf16[1280,1024]{1,0:T(8,128)(2,1)}, bf16[1280,1024]{1,0:T(8,128)(2,1)}, bf16[1...) custom-call(bf16[1,5,16,16,1024]{4,3,2,1,0:T(8,128)(2,1)} %x_hbm.1, ...), custom_call_target="tpu_custom_call" | custom-call | flops 9395240960 | bytes 26214400 | tf_op jit(solution)/shard_map/pre/pallas_call | solution.py:149
  29.8 27.8 %attn_fwd.1 = (bf16[1280,1024]{1,0:T(8,128)(2,1)}, f32[8,6,8,384]{3,2,1,0:T(8,128)}) custom-call(s32[1,2]{1,0:T(1,128)} %live_ref.7, bf16[1280,1024]{1,0:T(8,128)(2,1)} %get-tuple-element.43.q_ref, bf16[1280,1024]{1,0:T(8,128)(2,1)} %get-tuple-element.44.k_ref, bf16[1280,1024]{1,0:T(8,128)(2,1)} %get-tuple-element.45.v_ref, ...), custom_call_target="tpu_custom_call" | custom-call | flops 1677721600 | bytes 15728640 | tf_op jit(solution)/shard_map/attn_fwd/pallas_call | solution.py:465
  57.6 10.7 %mid.1 = (bf16[1280,1024]{1,0:T(8,128)(2,1)}, f32[1280,1024]{1,0:T(8,128)}, bf16[1280,1024]{1,0:T(8,128)(2,1)}, bf16[1024,1280]{1,0:T(8,128)(2,1)}, bf16[1024,1280]{1,0:T(8,128)(2,1)}) custom-call(s32[1,2]{1,0:T(1,128)} %live_ref.7, bf16[1280,1024]{1,0:T(8,128)(2,1)} %get-tuple-element.48.att_ref, bf16[1024,1024]{1,0:T(8,128)(2,1)} %wo_hbm.1, ...), custom_call_target="tpu_custom_call" | custom-call | flops 2684354560 | bytes 20971520 | tf_op jit(solution)/shard_map/mid/pallas_call | solution.py:497
  68.3 225.0 %core.1 = (bf16[1,5,16,16,1024]{4,3,2,1,0:T(8,128)(2,1)}, bf16[1,5,16,16,1024]{4,3,2,1,0:T(8,128)(2,1)}, f32[8,1024]{1,0:T(8,128)}, bf16[8,2,4,64,1024]{4,3,2,1,...) custom-call(s32[1,2]{1,0:T(1,128)} %live_ref.7, ...), custom_call_target="tpu_custom_call" | custom-call | flops 85563801600 | bytes 112197632 | tf_op jit(solution)/shard_map/core/pallas_call | solution.py:883
  293.3 7.6 %results.1 = (bf16[1,5,16,16,1024]{4,3,2,1,0:T(8,128)(2,1)}, bf16[1,5,16,16,1024]{4,3,2,1,0:T(8,128)(2,1)}, f32[1,6,1024]{2,1,0:T(8,128)}, f32[512,128]{1,0:T(8,...) custom-call(bf16[1,5,16,16,1024]{4,3,2,1,0:T(8,128)(2,1)} %get-tuple, ...), custom_call_target="tpu_custom_call" | custom-call | bytes 10485760 | tf_op jit(solution)/shard_map/results/pallas_call | solution.py:952
  300.9 1.4 copy.19
